TPU v7x, 32 devices: a whole 2x2x4 slice. The times are simulated.
32 devices in a mesh: run: 8 (over y, x, core), seg: 4 (over z).
Axes of the slice: x: 2, y: 2, z: 4, core: 2. Of those that a mesh axis runs over, the one named last changes fastest.
Arguments:
- diag_blocks: float32 [4, 16, 256, 256], P('seg', 'run'), as said below
- coupling: float32 [4, 16, 256, 256], P('seg', 'run')
- rhs: float32 [4, 16, 256, 128], P('seg', 'run'), may hold values from -0.65 to 0.65
Outputs:
- solution: float32 [4, 16, 256, 128], P('seg', 'run')
Inputs may be any that keep to these rules, and one draw needn't show every extreme that they name: Together with coupling, diag_blocks makes A symmetric positive definite.
All inputs are finite; a program needn't handle non-finite values.
Results may differ from a plain program's by a relative error of at most 0.0003.
Values sent between devices are 32-bit elements; how exact they have to be, the bound alone decides.
A program may use at most 128 MiB of HBM per device.

v0:
```python
import functools

import jax
import jax.numpy as jnp
from jax import lax
from jax.experimental import pallas as pl
from jax.experimental.pallas import tpu as pltpu
from jax.sharding import PartitionSpec as P

MESH = pl.DeviceIdType.MESH
HIGH = lax.Precision.HIGHEST
ROWS = 8
LANES = 128


def dot(a, b):
    return jnp.dot(a, b, precision=HIGH, preferred_element_type=jnp.float32)


def spd_inverse_tile(rows):
    count = len(rows)
    width = rows[0].shape[1]
    shape = (ROWS, width)
    sub = lax.broadcasted_iota(jnp.int32, shape, 0)
    lane = lax.broadcasted_iota(jnp.int32, shape, 1)
    rows = list(rows)
    for k in range(count):
        first = k * ROWS
        panel = rows[k]
        cols = [jnp.broadcast_to(panel[:, first + j : first + j + 1], shape) for j in range(ROWS)]
        for j in range(ROWS):
            here = sub == j
            pivot = jnp.broadcast_to(cols[j][j : j + 1, :], shape)
            inverse = 1.0 / pivot
            factor = jnp.where(here, -1.0, cols[j])
            panel = jnp.where(lane == first + j, jnp.where(here, 1.0, 0.0), panel)
            line = jnp.broadcast_to(panel[j : j + 1, :], shape)
            panel = jnp.where(here, 0.0, panel) - (factor * line) * inverse
            for m in range(j + 1, ROWS):
                line = jnp.broadcast_to(cols[m][j : j + 1, :], shape)
                cols[m] = jnp.where(here, 0.0, cols[m]) - (factor * line) * inverse
        lines = [jnp.broadcast_to(panel[j : j + 1, :], shape) for j in range(ROWS)]
        inside = jnp.logical_and(lane >= first, lane < first + ROWS)
        for i in range(count):
            if i == k:
                continue
            old = rows[i]
            terms = [
                jnp.broadcast_to(old[:, first + j : first + j + 1], shape) * lines[j]
                for j in range(ROWS)
            ]
            while len(terms) > 1:
                terms = [terms[t] + terms[t + 1] for t in range(0, len(terms), 2)]
            rows[i] = jnp.where(inside, 0.0, old) - terms[0]
        rows[k] = panel
    return rows


def invert_into(d_ref, x_ref, tile_ref, side_ref):
    order = d_ref.shape[0]
    blocks = order // LANES
    x_ref[...] = d_ref[...]

    @pl.loop(0, blocks)
    def _(step):
        for at in range(blocks):

            @pl.when(step == at)
            def _():
                own = slice(at * LANES, (at + 1) * LANES)
                tile_ref[...] = x_ref[own, own]

        tile = spd_inverse_tile([tile_ref[i : i + ROWS, :] for i in range(0, LANES, ROWS)])
        for i, row in enumerate(tile):
            tile_ref[i * ROWS : (i + 1) * ROWS, :] = row

        for at in range(blocks):

            @pl.when(step == at)
            def _():
                own = slice(at * LANES, (at + 1) * LANES)
                inverse = tile_ref[...]
                for other in range(blocks):
                    if other != at:
                        theirs = slice(other * LANES, (other + 1) * LANES)
                        side_ref[own, theirs] = dot(inverse, x_ref[own, theirs])
                for other in range(blocks):
                    if other == at:
                        continue
                    theirs = slice(other * LANES, (other + 1) * LANES)
                    link = x_ref[theirs, own]
                    for last in range(blocks):
                        if last != at:
                            there = slice(last * LANES, (last + 1) * LANES)
                            x_ref[theirs, there] = x_ref[theirs, there] - dot(
                                link, side_ref[own, there]
                            )
                    x_ref[theirs, own] = -dot(link, inverse)
                for other in range(blocks):
                    if other != at:
                        theirs = slice(other * LANES, (other + 1) * LANES)
                        x_ref[own, theirs] = side_ref[own, theirs]
                x_ref[own, own] = inverse


def kernel(
    runs,
    total,
    diag,
    coup,
    rhs,
    out,
    x,
    tile,
    side,
    node,
    source,
    link,
    turned,
    keep_e,
    keep_f,
    keep_y,
    send_d,
    send_m,
    send_b,
    first_d,
    first_b,
    got_d,
    got_b,
    got_low,
    got_up,
    above,
    below,
    before,
    value,
    sent,
    sent_first,
    sent_value,
    come_d,
    come_b,
    come_m,
    come_first,
    come_value,
):
    slabs = diag.shape[0]
    inner = slabs - 1
    me = lax.axis_index("seg") * runs + lax.axis_index("run")
    strides = [1 << i for i in range(total.bit_length() - 1)]
    root = me == total - 1
    even = lax.rem(me, 2) == 0

    def copy(source_ref, target_ref, send_sem, recv_sem, peer):
        return pltpu.make_async_remote_copy(
            src_ref=source_ref,
            dst_ref=target_ref,
            send_sem=send_sem,
            recv_sem=recv_sem,
            device_id=(lax.rem(peer, runs), lax.div(peer, runs)),
            device_id_type=MESH,
        )

    barrier = pltpu.get_barrier_semaphore()
    met = [lax.rem(me + 1, s) == 0 for s in strides]
    peers = sum(
        jnp.where(jnp.logical_and(here, ok), 1, 0)
        for s, here in zip(strides, met)
        for ok in (me >= s, me + s < total)
    )
    for s, here in zip(strides, met):
        for ok, peer in ((me >= s, me - s), (me + s < total, me + s)):

            @pl.when(jnp.logical_and(here, ok))
            def _():
                pl.semaphore_signal(
                    barrier,
                    inc=1,
                    device_id=(lax.rem(peer, runs), lax.div(peer, runs)),
                    device_id_type=MESH,
                )

    link[...] = jnp.where(me == 0, jnp.zeros_like(coup[0]), coup[0])
    node[...] = diag[0]
    source[...] = rhs[0]
    for i in range(inner):
        invert_into(node, x, tile, side)
        f_turned = coup[i + 1]
        turned[...] = link[...].T
        keep_e[i] = dot(x[...], link[...])
        keep_f[i] = dot(x[...], f_turned.T)
        term = dot(turned[...], keep_e[i])
        first_d[...] = -term if i == 0 else first_d[...] - term
        node[...] = diag[i + 1] - dot(f_turned, keep_f[i])
        if i == inner - 1:
            pl.semaphore_wait(barrier, peers)

            @pl.when(me > 0)
            def _():
                copy(first_d, got_d.at[0], sent_first.at[0], come_first.at[0], me - 1).start()

            @pl.when(jnp.logical_not(even))
            def _():
                send_m[...] = -dot(turned[...], keep_f[i])
                copy(send_m, got_up, sent_first.at[1], come_m.at[1], me - 1).start()

        keep_y[i] = dot(x[...], source[...])
        term = dot(turned[...], keep_y[i])
        first_b[...] = -term if i == 0 else first_b[...] - term
        if i == inner - 1:

            @pl.when(me > 0)
            def _():
                copy(first_b, got_b.at[0], sent_first.at[2], come_first.at[1], me - 1).start()

        source[...] = rhs[i + 1] - dot(f_turned, keep_y[i])
        link[...] = -dot(f_turned, keep_e[i])

    @pl.when(jnp.logical_not(root))
    def _():
        copy(first_d, got_d.at[0], sent_first.at[0], come_first.at[0], me + 1).wait_recv()
        node[...] = node[...] + got_d[0]

    for i, s in enumerate(strides):
        for way, (ok, peer) in enumerate(((me >= s, me - s), (me + s < total, me + s))):

            @pl.when(jnp.logical_and(lax.rem(me + 1, 2 * s) == 0, ok))
            def _():
                slot = 1 + 2 * i + way
                copy(
                    first_d, got_d.at[slot], sent_first.at[0], come_d.at[2 * i + way], peer
                ).wait_recv()
                node[...] = node[...] + got_d[slot]

    @pl.when(jnp.logical_not(even))
    def _():
        copy(send_m, got_up, sent_first.at[1], come_m.at[1], me - 1).wait_send()

    invert_into(node, x, tile, side)

    @pl.when(jnp.logical_not(root))
    def _():
        copy(first_b, got_b.at[0], sent_first.at[2], come_first.at[1], me + 1).wait_recv()
        source[...] = source[...] + got_b[0]

    for i, s in enumerate(strides):
        for way, (ok, peer) in enumerate(((me >= s, me - s), (me + s < total, me + s))):

            @pl.when(jnp.logical_and(lax.rem(me + 1, 2 * s) == 0, ok))
            def _():
                slot = 1 + 2 * i + way
                copy(
                    first_b, got_b.at[slot], sent_first.at[2], come_b.at[2 * i + way], peer
                ).wait_recv()
                source[...] = source[...] + got_b[slot]

    @pl.when(jnp.logical_not(root))
    def _():
        copy(send_m, got_up, sent_first.at[1], come_m.at[1], me + 1).wait_recv()

        @pl.when(jnp.logical_not(even))
        def _():
            copy(send_m, got_low, sent_first.at[1], come_m.at[0], me - 1).wait_recv()
            link[...] = got_low[...]

        turned[...] = got_up[...].T
        keep_f[inner] = dot(x[...], got_up[...])
        send_d[1] = -dot(turned[...], keep_f[inner])

    def sends(stage, act):
        for i, s in enumerate(strides):
            mine = lax.rem(me, 2 * s) == s - 1
            lower = jnp.logical_and(mine, me >= s)
            to_low = jnp.logical_and(lax.rem(me + s, 4 * s) == 2 * s - 1, me + s < total - 1)
            if stage == "up":

                @pl.when(mine)
                def _():
                    act(copy(send_d.at[1], got_d.at[1 + 2 * i], sent.at[0], come_d.at[2 * i], me + s))

            if stage == "down":

                @pl.when(lower)
                def _():
                    act(
                        copy(
                            send_d.at[0],
                            got_d.at[2 + 2 * i],
                            sent.at[1],
                            come_d.at[2 * i + 1],
                            me - s,
                        )
                    )

            if stage == "link":

                @pl.when(jnp.logical_and(mine, to_low))
                def _():
                    act(copy(send_m, got_low, sent.at[2], come_m.at[0], me + s))

                @pl.when(jnp.logical_and(lower, lax.rem(me + s, 4 * s) == 4 * s - 1))
                def _():
                    act(copy(send_m, got_up, sent.at[2], come_m.at[1], me - s))

            if stage == "thin":

                @pl.when(mine)
                def _():
                    act(copy(send_b.at[1], got_b.at[1 + 2 * i], sent.at[3], come_b.at[2 * i], me + s))

                @pl.when(lower)
                def _():
                    act(
                        copy(
                            send_b.at[0],
                            got_b.at[2 + 2 * i],
                            sent.at[4],
                            come_b.at[2 * i + 1],
                            me - s,
                        )
                    )

    start = lambda c: c.start()
    done = lambda c: c.wait_send()
    sends("up", start)

    @pl.when(jnp.logical_not(root))
    def _():
        side[...] = link[...].T
        keep_e[inner] = dot(x[...], link[...])
        send_d[0] = -dot(side[...], keep_e[inner])

    sends("down", start)
    next_above = functools.reduce(
        jnp.logical_or,
        [
            jnp.logical_and(
                lax.rem(me, 2 * s) == s - 1, lax.rem(me + s, 4 * s) == 2 * s - 1
            )
            for s in strides
        ],
    )

    @pl.when(next_above)
    def _():
        send_m[...] = -dot(turned[...], keep_e[inner])

    @pl.when(jnp.logical_not(next_above))
    def _():
        send_m[...] = -dot(side[...], keep_f[inner])

    sends("link", start)
    keep_y[inner] = dot(x[...], source[...])
    value[...] = keep_y[inner]

    @pl.when(jnp.logical_not(root))
    def _():
        send_b[1] = -dot(turned[...], keep_y[inner])
        send_b[0] = -dot(side[...], keep_y[inner])

    sends("thin", start)

    for i, s in enumerate(strides):
        mine = lax.rem(me, 2 * s) == s - 1

        @pl.when(jnp.logical_and(mine, me >= s))
        def _():
            copy(value, below, sent_value.at[0], come_value.at[0], me - s).wait_recv()
            value[...] = value[...] - dot(keep_e[inner], below[...])

        @pl.when(mine)
        def _():
            copy(value, above, sent_value.at[0], come_value.at[1], me + s).wait_recv()
            value[...] = value[...] - dot(keep_f[inner], above[...])

    def hand_down(act):
        for i, s in reversed(list(enumerate(strides))):
            parent = lax.rem(me + 1, 2 * s) == 0

            @pl.when(parent)
            def _():
                act(copy(value, above, sent_value.at[2 * i], come_value.at[1], me - s))

            @pl.when(jnp.logical_and(parent, me + s < total))
            def _():
                act(copy(value, below, sent_value.at[2 * i + 1], come_value.at[0], me + s))

        @pl.when(even)
        def _():
            act(copy(value, before, sent_value.at[2 * len(strides)], come_value.at[2], me + 1))

    hand_down(start)
    out[inner] = value[...]
    for i in reversed(range(inner)):
        out[i] = keep_y[i] - dot(keep_f[i], out[i + 1])

    @pl.when(jnp.logical_and(even, me > 0))
    def _():
        for i in reversed(range(inner)):
            out[i] = out[i] - dot(keep_e[i], below[...])

    @pl.when(jnp.logical_not(even))
    def _():
        copy(value, before, sent_value.at[2 * len(strides)], come_value.at[2], me - 1).wait_recv()
        for i in reversed(range(inner)):
            out[i] = out[i] - dot(keep_e[i], before[...])

    for stage in ("up", "down", "link", "thin"):
        sends(stage, done)
    hand_down(done)

    @pl.when(me > 0)
    def _():
        copy(first_d, got_d.at[0], sent_first.at[0], come_first.at[0], me - 1).wait_send()
        copy(first_b, got_b.at[0], sent_first.at[2], come_first.at[1], me - 1).wait_send()


def local(runs, total, diag_blocks, coupling, rhs):
    slabs, order = diag_blocks.shape[1:3]
    columns = rhs.shape[3]
    depth = total.bit_length() - 1
    square, thin = (order, order), (order, columns)
    vmem = lambda *shape: pltpu.VMEM(shape, jnp.float32)
    dma = lambda n: pltpu.SemaphoreType.DMA((n,))
    result = pl.pallas_call(
        functools.partial(kernel, runs, total),
        out_shape=jax.ShapeDtypeStruct(rhs.shape[1:], jnp.float32),
        in_specs=[pl.BlockSpec(memory_space=pltpu.VMEM)] * 3,
        out_specs=pl.BlockSpec(memory_space=pltpu.VMEM),
        scratch_shapes=[
            vmem(*square),
            vmem(LANES, LANES),
            vmem(*square),
            vmem(*square),
            vmem(*thin),
            vmem(*square),
            vmem(*square),
            vmem(slabs, *square),
            vmem(slabs, *square),
            vmem(slabs, *thin),
            vmem(2, *square),
            vmem(*square),
            vmem(2, *thin),
            vmem(*square),
            vmem(*thin),
            vmem(1 + 2 * depth, *square),
            vmem(1 + 2 * depth, *thin),
            vmem(*square),
            vmem(*square),
            vmem(*thin),
            vmem(*thin),
            vmem(*thin),
            vmem(*thin),
            dma(5),
            dma(3),
            dma(2 * depth + 1),
            dma(2 * depth),
            dma(2 * depth),
            dma(2),
            dma(2),
            dma(3),
        ],
        compiler_params=pltpu.CompilerParams(collective_id=0, has_side_effects=True),
        name="chain_solve",
    )(diag_blocks[0], coupling[0], rhs[0])
    return result[None]


def solution(mesh):
    spec = P("seg", "run", None, None)
    runs = mesh.shape["run"]
    total = runs * mesh.shape["seg"]
    return jax.shard_map(
        functools.partial(local, runs, total),
        mesh=mesh,
        in_specs=(spec, spec, spec),
        out_specs=spec,
        check_vma=False,
    )
```

profile of v0, /device:TPU:15, one launch (start us, length us, event | category | flops | bytes accessed | tf_op | source)
XLA Modules:
  0.0 141.2 jit_solution(16242680528414174189)
XLA Ops:
  0.0 139.5 %chain_solve.1 = f32[2,256,128]{2,1,0:T(8,128)} custom-call(f32[2,256,256]{2,1,0:T(8,128)} %bitcast.5, f32[2,256,256]{2,1,0:T(8,128)} %bitcast.6, f32[2,256,128]{2,1,0:T(8,128)} %bitcast.7), custom_call_target="tpu_custom_call" | custom-call | tf_op jit(solution)/shard_map/chain_solve/pallas_call | solution.py:423
  139.5 1.7 %copy.5 = f32[1,2,256,128]{3,2,1,0:T(8,128)} copy(f32[1,2,256,128]{3,2,1,0:T(8,128)} %bitcast.4) | data formatting | bytes 524288
where the time goes:
time: 141 us
  Pallas kernels  139 us (99%)
  local copies, waits for them, and re-layouts  1.67 us (1%)
    pallas_call x1, Pallas kernels, local(): pl.pallas_call(functools.partial(kernel, runs, total), out_shape=jax.Shap...  139 us

commit v1 on v0

v1 whole, which is shorter than its diff:
```python
import functools

import jax
import jax.numpy as jnp
from jax import lax
from jax.experimental import pallas as pl
from jax.experimental.pallas import tpu as pltpu
from jax.sharding import PartitionSpec as P

MESH = pl.DeviceIdType.MESH
HIGH = lax.Precision.HIGHEST
ROWS = 8
LANES = 128


def dot(a, b):
    return jnp.dot(a, b, precision=HIGH, preferred_element_type=jnp.float32)


def dot_nt(a, b):
    return lax.dot_general(
        a, b, (((1,), (1,)), ((), ())), precision=HIGH, preferred_element_type=jnp.float32
    )


def spd_inverse_tile(rows):
    count = len(rows)
    width = rows[0].shape[1]
    shape = (ROWS, width)
    sub = lax.broadcasted_iota(jnp.int32, shape, 0)
    lane = lax.broadcasted_iota(jnp.int32, shape, 1)
    rows = list(rows)
    for k in range(count):
        first = k * ROWS
        panel = rows[k]
        cols = [jnp.broadcast_to(panel[:, first + j : first + j + 1], shape) for j in range(ROWS)]
        for j in range(ROWS):
            here = sub == j
            pivot = jnp.broadcast_to(cols[j][j : j + 1, :], shape)
            inverse = 1.0 / pivot
            factor = jnp.where(here, -1.0, cols[j])
            panel = jnp.where(lane == first + j, jnp.where(here, 1.0, 0.0), panel)
            line = jnp.broadcast_to(panel[j : j + 1, :], shape)
            panel = jnp.where(here, 0.0, panel) - (factor * line) * inverse
            for m in range(j + 1, ROWS):
                line = jnp.broadcast_to(cols[m][j : j + 1, :], shape)
                cols[m] = jnp.where(here, 0.0, cols[m]) - (factor * line) * inverse
        lines = [jnp.broadcast_to(panel[j : j + 1, :], shape) for j in range(ROWS)]
        inside = jnp.logical_and(lane >= first, lane < first + ROWS)
        for i in range(count):
            if i == k:
                continue
            old = rows[i]
            terms = [
                jnp.broadcast_to(old[:, first + j : first + j + 1], shape) * lines[j]
                for j in range(ROWS)
            ]
            while len(terms) > 1:
                terms = [terms[t] + terms[t + 1] for t in range(0, len(terms), 2)]
            rows[i] = jnp.where(inside, 0.0, old) - terms[0]
        rows[k] = panel
    return rows


def invert(node, x, tile, work, late):
    half = tile.shape[0]
    top, low = slice(0, half), slice(half, 2 * half)
    tile[...] = node[0]

    @pl.loop(0, 2)
    def _(step):
        rows = spd_inverse_tile([tile[i : i + ROWS, :] for i in range(0, half, ROWS)])
        for i, row in enumerate(rows):
            tile[i * ROWS : (i + 1) * ROWS, :] = row

        @pl.when(step == 0)
        def _():
            late()
            x[top, top] = tile[...]
            work[0] = dot(tile[...], node[1])
            work[1] = work[0].T
            tile[...] = node[2] - dot(work[1], node[1])

        @pl.when(step == 1)
        def _():
            corner = -dot(tile[...], work[1])
            x[low, low] = tile[...]
            x[low, top] = corner
            x[top, low] = -dot(work[0], tile[...])
            x[top, top] = x[top, top] - dot(work[0], corner)


def kernel(
    runs,
    total,
    diag,
    coup,
    rhs,
    out,
    x,
    tile,
    work,
    node,
    source,
    e_turned,
    w_p,
    w_q,
    keep_p,
    keep_q,
    keep_y,
    send_d,
    send_m,
    send_b,
    first_d,
    first_b,
    got_d,
    got_b,
    got_link,
    got_x,
    before,
    value,
    sent,
    sent_first,
    sent_value,
    come_d,
    come_b,
    come_m,
    come_x,
):
    slabs, order = diag.shape[:2]
    inner = slabs - 1
    half = order // 2
    top, low = slice(0, half), slice(half, order)
    me = lax.axis_index("seg") * runs + lax.axis_index("run")
    depth = total.bit_length() - 1
    strides = [1 << i for i in range(depth)]
    root = me == total - 1
    inside = jnp.logical_not(root)
    even = lax.rem(me, 2) == 0
    odd = jnp.logical_not(even)
    parents = [lax.rem(me + 1, 2 * s) == 0 for s in strides]
    level = sum(jnp.where(parent, 1, 0) for parent in parents)
    span = 1 + sum(jnp.where(parent, s, 0) for s, parent in zip(strides, parents))
    next_above = lax.rem(me + span, 4 * span) == 2 * span - 1
    up = jnp.where(next_above, 1, 0)
    peer_p = jnp.where(next_above, me + span, me - span)
    peer_q = jnp.where(next_above, me - span, me + span)
    has_q = jnp.logical_and(inside, jnp.logical_and(peer_q >= 0, peer_q < total))
    slot_p = 1 + 2 * level + (1 - up)
    slot_q = 1 + 2 * level + up

    def copy(source_ref, target_ref, send_sem, recv_sem, peer):
        return pltpu.make_async_remote_copy(
            src_ref=source_ref,
            dst_ref=target_ref,
            send_sem=send_sem,
            recv_sem=recv_sem,
            device_id=(lax.rem(peer, runs), lax.div(peer, runs)),
            device_id_type=MESH,
        )

    barrier = pltpu.get_barrier_semaphore()
    met = [lax.rem(me + 1, s) == 0 for s in strides]
    peers = sum(
        jnp.where(jnp.logical_and(here, ok), 1, 0)
        for s, here in zip(strides, met)
        for ok in (me >= s, me + s < total)
    )
    for s, here in zip(strides, met):
        for ok, peer in ((me >= s, me - s), (me + s < total, me + s)):

            @pl.when(jnp.logical_and(here, ok))
            def _():
                pl.semaphore_signal(
                    barrier,
                    inc=1,
                    device_id=(lax.rem(peer, runs), lax.div(peer, runs)),
                    device_id_type=MESH,
                )

    def first_head(peer):
        return copy(first_d.at[0], got_d.at[0, 0], sent_first.at[0], come_d.at[0], peer)

    def first_tail(peer):
        return copy(
            first_d.at[pl.ds(1, 2)], got_d.at[0, pl.ds(1, 2)], sent_first.at[1], come_d.at[1], peer
        )

    def first_link(peer):
        return copy(send_m, got_link.at[1], sent_first.at[2], come_m.at[1], peer)

    def first_thin(peer):
        return copy(first_b, got_b.at[0], sent_first.at[3], come_b.at[0], peer)

    def head(role, slot, peer):
        return copy(
            send_d.at[role, 0], got_d.at[slot, 0], sent.at[role], come_d.at[2 * slot], peer
        )

    def tail(role, slot, peer):
        return copy(
            send_d.at[role, pl.ds(1, 2)],
            got_d.at[slot, pl.ds(1, 2)],
            sent.at[2 + role],
            come_d.at[2 * slot + 1],
            peer,
        )

    def thin(role, slot, peer):
        return copy(send_b.at[role], got_b.at[slot], sent.at[4 + role], come_b.at[slot], peer)

    def coupled(side, peer):
        return copy(send_m, got_link.at[side], sent.at[6], come_m.at[side], peer)

    def each_source(act):
        @pl.when(inside)
        def _():
            act(0, me + 1)

        for i, s in enumerate(strides):
            for way, (ok, peer) in enumerate(((me >= s, me - s), (me + s < total, me + s))):

                @pl.when(jnp.logical_and(parents[i], ok))
                def _():
                    act(1 + 2 * i + way, peer)

    e_turned[...] = jnp.where(me == 0, jnp.zeros_like(coup[0]), coup[0]).T
    node[0] = diag[0, top, top]
    node[1] = diag[0, top, low]
    node[2] = diag[0, low, low]
    source[...] = rhs[0]
    for i in range(inner):
        final = i == inner - 1
        f_turned = coup.at[i + 1]
        invert(node, x, tile, work, lambda: None)
        w_p[...] = dot(e_turned[...], x[...])

        def put(block, rows, columns):
            term = dot_nt(w_p[rows, :], e_turned[columns, :])
            first_d[block] = -term if i == 0 else first_d[block] - term

        put(0, top, top)
        if final:
            pl.semaphore_wait(barrier, peers)

            @pl.when(me > 0)
            def _():
                first_head(me - 1).start()

        put(1, top, low)
        put(2, low, low)
        if final:

            @pl.when(me > 0)
            def _():
                first_tail(me - 1).start()

        w_q[...] = dot(f_turned[...], x[...])
        node[0] = diag[i + 1, top, top] - dot_nt(w_q[top, :], f_turned[top, :])
        node[1] = diag[i + 1, top, low] - dot_nt(w_q[top, :], f_turned[low, :])
        node[2] = diag[i + 1, low, low] - dot_nt(w_q[low, :], f_turned[low, :])
        if final:

            @pl.when(odd)
            def _():
                send_m[...] = -dot_nt(w_q[...], e_turned[...])
                first_link(me - 1).start()

            @pl.when(even)
            def _():
                got_link[0] = -dot_nt(w_p[...], f_turned[...])

        keep_y[i] = dot(x[...], source[...])
        term = dot(e_turned[...], keep_y[i])
        first_b[...] = -term if i == 0 else first_b[...] - term
        if final:

            @pl.when(me > 0)
            def _():
                first_thin(me - 1).start()

        source[...] = rhs[i + 1] - dot(f_turned[...], keep_y[i])
        keep_p[i] = dot_nt(x[...], e_turned[...])
        keep_q[i] = dot_nt(x[...], f_turned[...])
        if not final:
            e_turned[...] = -dot_nt(w_p[...], f_turned[...])

    def add_head(slot, peer):
        head(0, slot, peer).wait_recv()
        node[0] = node[0] + got_d[slot, 0]

    def add_tail(slot, peer):
        tail(0, slot, peer).wait_recv()
        node[1] = node[1] + got_d[slot, 1]
        node[2] = node[2] + got_d[slot, 2]

    def add_thin(slot, peer):
        thin(0, slot, peer).wait_recv()
        source[...] = source[...] + got_b[slot]

    each_source(add_head)
    invert(node, x, tile, work, lambda: each_source(add_tail))

    @pl.when(inside)
    def _():
        coupled(1, me + 1).wait_recv()

        @pl.when(odd)
        def _():
            coupled(0, me - 1).wait_recv()
            first_link(me - 1).wait_send()

        def serve(role, slot, peer, weights, turned):
            weights[top, :] = dot(turned[top, :], x[...])
            send_d[role, 0] = -dot_nt(weights[top, :], turned[top, :])
            go = inside if role == 0 else has_q

            @pl.when(go)
            def _():
                head(role, slot, peer).start()

            send_d[role, 1] = -dot_nt(weights[top, :], turned[low, :])
            weights[low, :] = dot(turned[low, :], x[...])
            send_d[role, 2] = -dot_nt(weights[low, :], turned[low, :])

            @pl.when(go)
            def _():
                tail(role, slot, peer).start()

        serve(0, slot_p, peer_p, w_p, got_link.at[up])
        serve(1, slot_q, peer_q, w_q, got_link.at[1 - up])

        @pl.when(peer_p < total - 1)
        def _():
            send_m[...] = -dot_nt(w_q[...], got_link[up])
            coupled(1 - up, peer_p).start()

    each_source(add_thin)
    keep_y[inner] = dot(x[...], source[...])
    value[...] = keep_y[inner]

    @pl.when(inside)
    def _():
        send_b[0] = -dot(got_link[up], keep_y[inner])
        thin(0, slot_p, peer_p).start()

        @pl.when(has_q)
        def _():
            send_b[1] = -dot(got_link[1 - up], keep_y[inner])
            thin(1, slot_q, peer_q).start()

        keep_p[inner] = dot_nt(x[...], got_link[up])
        keep_q[inner] = dot_nt(x[...], got_link[1 - up])

        @pl.when(has_q)
        def _():
            copy(value, got_x.at[1], sent_value.at[0], come_x.at[1], peer_q).wait_recv()
            value[...] = value[...] - dot(keep_q[inner], got_x[1])

        copy(value, got_x.at[0], sent_value.at[0], come_x.at[0], peer_p).wait_recv()
        value[...] = value[...] - dot(keep_p[inner], got_x[0])

    def hand_down(act):
        for i, s in reversed(list(enumerate(strides))):
            role = jnp.where(level == i + 1, 0, 1)
            for way, (ok, peer) in enumerate(((me >= s, me - s), (me + s < total, me + s))):

                @pl.when(jnp.logical_and(parents[i], ok))
                def _():
                    act(
                        copy(
                            value, got_x.at[role], sent_value.at[2 * i + way], come_x.at[role], peer
                        )
                    )

        @pl.when(even)
        def _():
            act(copy(value, before, sent_value.at[2 * depth], come_x.at[2], me + 1))

    hand_down(lambda c: c.start())
    out[inner] = value[...]
    for i in reversed(range(inner)):
        out[i] = keep_y[i] - dot(keep_q[i], out[i + 1])

    @pl.when(jnp.logical_and(even, me > 0))
    def _():
        for i in reversed(range(inner)):
            out[i] = out[i] - dot(keep_p[i], got_x[up])

    @pl.when(odd)
    def _():
        copy(value, before, sent_value.at[2 * depth], come_x.at[2], me - 1).wait_recv()
        for i in reversed(range(inner)):
            out[i] = out[i] - dot(keep_p[i], before[...])

    @pl.when(inside)
    def _():
        head(0, slot_p, peer_p).wait_send()
        tail(0, slot_p, peer_p).wait_send()
        thin(0, slot_p, peer_p).wait_send()

        @pl.when(peer_p < total - 1)
        def _():
            coupled(1 - up, peer_p).wait_send()

        @pl.when(has_q)
        def _():
            head(1, slot_q, peer_q).wait_send()
            tail(1, slot_q, peer_q).wait_send()
            thin(1, slot_q, peer_q).wait_send()

    hand_down(lambda c: c.wait_send())

    @pl.when(me > 0)
    def _():
        first_head(me - 1).wait_send()
        first_tail(me - 1).wait_send()
        first_thin(me - 1).wait_send()

    @pl.when(jnp.logical_and(odd, root))
    def _():
        first_link(me - 1).wait_send()


def local(runs, total, diag_blocks, coupling, rhs):
    slabs, order = diag_blocks.shape[1:3]
    half = order // 2
    columns = rhs.shape[3]
    depth = total.bit_length() - 1
    square, thin = (order, order), (order, columns)
    vmem = lambda *shape: pltpu.VMEM(shape, jnp.float32)
    dma = lambda n: pltpu.SemaphoreType.DMA((n,))
    slots = 1 + 2 * depth
    result = pl.pallas_call(
        functools.partial(kernel, runs, total),
        out_shape=jax.ShapeDtypeStruct(rhs.shape[1:], jnp.float32),
        in_specs=[pl.BlockSpec(memory_space=pltpu.VMEM)] * 3,
        out_specs=pl.BlockSpec(memory_space=pltpu.VMEM),
        scratch_shapes=[
            vmem(*square),
            vmem(half, half),
            vmem(2, half, half),
            vmem(3, half, half),
            vmem(*thin),
            vmem(*square),
            vmem(*square),
            vmem(*square),
            vmem(slabs, *square),
            vmem(slabs, *square),
            vmem(slabs, *thin),
            vmem(2, 3, half, half),
            vmem(*square),
            vmem(2, *thin),
            vmem(3, half, half),
            vmem(*thin),
            vmem(slots, 3, half, half),
            vmem(slots, *thin),
            vmem(2, *square),
            vmem(2, *thin),
            vmem(*thin),
            vmem(*thin),
            dma(7),
            dma(4),
            dma(slots),
            dma(2 * slots),
            dma(slots),
            dma(2),
            dma(3),
        ],
        compiler_params=pltpu.CompilerParams(collective_id=0, has_side_effects=True),
        name="chain_solve",
    )(diag_blocks[0], coupling[0], rhs[0])
    return result[None]


def solution(mesh):
    spec = P("seg", "run", None, None)
    runs = mesh.shape["run"]
    total = runs * mesh.shape["seg"]
    return jax.shard_map(
        functools.partial(local, runs, total),
        mesh=mesh,
        in_specs=(spec, spec, spec),
        out_specs=spec,
        check_vma=False,
    )
```

time: 141 us -> 119 us (0.84)
  Pallas kernels: 139 us -> 117 us
    pallas_call x1, Pallas kernels: 139 us -> 117 us  [local(): pl.pallas_call(functools.partial(kernel, runs, total), out_shape=jax.Shap...]
where the time goes in v1:
time: 119 us; the launch traced here: 118 us
  Pallas kernels  117 us (98%)
  local copies, waits for them, and re-layouts  1.67 us (1%)
    pallas_call x1, Pallas kernels, local(): pl.pallas_call(functools.partial(kernel, runs, total), out_shape=jax.Shap...  117 us

profile of v1, /device:TPU:15, one launch (start us, length us, event | category | flops | bytes accessed | tf_op | source)
XLA Modules:
  0.0 118.4 jit_solution(13026823276894908219)
XLA Ops:
  0.0 116.7 %chain_solve.1 = f32[2,256,128]{2,1,0:T(8,128)} custom-call(f32[2,256,256]{2,1,0:T(8,128)} %bitcast.5, f32[2,256,256]{2,1,0:T(8,128)} %bitcast.6, f32[2,256,128]{2,1,0:T(8,128)} %bitcast.7), custom_call_target="tpu_custom_call" | custom-call | tf_op jit(solution)/shard_map/chain_solve/pallas_call | solution.py:434
  116.7 1.7 %copy.5 = f32[1,2,256,128]{3,2,1,0:T(8,128)} copy(f32[1,2,256,128]{3,2,1,0:T(8,128)} %bitcast.4) | data formatting | bytes 524288
